TPU v7x, 256 devices: a whole 4x4x8 slice. The times are simulated.
256 devices in a mesh: tok: 32 (over y, x, core), rep: 8 (over z).
Axes of the slice: x: 4, y: 4, z: 8, core: 2. Of those that a mesh axis runs over, the one named last changes fastest.
Arguments:
- hidden_states: bfloat16 [8, 4096, 2048], P('rep', 'tok'), may hold values from -6 to 6
- routes: int32 [8, 4096, 8], P('rep', 'tok'), may hold values from 0 to 31, all different within a row; in each aligned block of 128 rows (0 to 127, 128 to 255, ..., all dimensions but the last counted through in order) at most 36 rows name the same one
- gate_prob: float32 [8, 4096, 8], P('rep', 'tok'), may hold values from 0.03 to 0.3
- gate_up: float32 [32, 2048, 2048], P('tok', 'rep'), may hold values from -0.125 to 0.125
- down: float32 [32, 1024, 2048], P('tok', 'rep'), may hold values from -0.1875 to 0.1875
Outputs:
- mixed: bfloat16 [8, 4096, 2048], P('rep', 'tok')
Inputs may be any that keep to these rules, and one draw needn't show every extreme that they name: `routes`: each row names 8 different experts. No expert is named by more than 36 rows of one device's 128 tokens, and some expert reaches 36 on some devices.
All inputs are finite; a program needn't handle non-finite values.
Results may differ from a plain program's by a relative error of at most 0.012.
Values may be sent and summed in bfloat16 or wider, within the bound.
No kernel may reach another device: no remote copies, remote signals or barrier semaphores. Data moves between devices by JAX's collectives and lax.ppermute only.
A program may use at most 128 MiB of HBM per device.

v0:
```python
import jax
import jax.numpy as jnp
from jax import lax
from jax.sharding import PartitionSpec as P

CAP = 36


def per_device(hidden_states, routes, gate_prob, gate_up, down):
    groups = lax.axis_size("tok")
    local_experts = gate_up.shape[0]
    model_width = hidden_states.shape[2]
    token_count = hidden_states.shape[1]
    top_count = routes.shape[2]
    all_experts = groups * local_experts
    capacity = CAP
    served_gate = gate_up.astype(jnp.bfloat16)
    served_down = down.astype(jnp.bfloat16)
    unit_count = served_gate.shape[2] // 2
    full_gate, full_down = (
        lax.all_gather(served_gate, "rep", axis=1, tiled=True),
        lax.all_gather(served_down, "rep", axis=1, tiled=True),
    )
    flat_picks = routes[0].reshape(-1)
    pick_count = flat_picks.shape[0]
    one_hot = (flat_picks[:, None] == jnp.arange(all_experts, dtype=jnp.int32)[None, :]).astype(
        jnp.int32
    )
    earlier = jnp.cumsum(one_hot, axis=0) - one_hot
    slot_index = jnp.sum(earlier * one_hot, axis=1)
    owners = jnp.arange(pick_count, dtype=jnp.int32) // top_count
    slot_table = (
        jnp.full((all_experts, capacity), token_count, jnp.int32)
        .at[flat_picks, slot_index]
        .set(owners)
    )
    padded_rows = jnp.concatenate(
        [hidden_states[0], jnp.zeros((1, model_width), jnp.bfloat16)], axis=0
    )
    send_rows = padded_rows[slot_table].reshape(groups, local_experts, capacity, model_width)
    arrived = lax.all_to_all(send_rows, "tok", split_axis=0, concat_axis=0, tiled=True)
    gate_both = jnp.einsum("secd,edf->secf", arrived, full_gate, preferred_element_type=jnp.float32)
    hidden_units = (jax.nn.silu(gate_both[..., :unit_count]) * gate_both[..., unit_count:]).astype(
        jnp.bfloat16
    )
    projected = jnp.einsum(
        "secf,efd->secd", hidden_units, full_down, preferred_element_type=jnp.float32
    )
    expert_out = projected.astype(jnp.bfloat16)
    returned = lax.all_to_all(expert_out, "tok", split_axis=0, concat_axis=0, tiled=True)
    returned = returned.reshape(all_experts, capacity, model_width)
    picked_rows = returned[flat_picks, slot_index].reshape(token_count, top_count, model_width)
    mixed_rows = jnp.einsum(
        "tk,tkd->td", gate_prob[0], picked_rows, preferred_element_type=jnp.float32
    )
    return mixed_rows.astype(jnp.bfloat16)[None]


def solution(mesh):
    return jax.shard_map(
        per_device,
        mesh=mesh,
        in_specs=(
            P("rep", "tok", None),
            P("rep", "tok", None),
            P("rep", "tok", None),
            P("tok", "rep", None),
            P("tok", "rep", None),
        ),
        out_specs=P("rep", "tok", None),
        check_vma=False,
    )
```

profile of v0, /device:TPU:7, one launch (start us, length us, event | category | flops | bytes accessed | tf_op | source)
XLA Modules:
  0.0 288.8 jit_solution(6611978452512759054)
XLA Ops:
  6.5 0.0 copy-start.4
  6.5 0.0 copy-start.3
  6.5 0.0 copy-start.1
  6.5 0.0 all-gather.3.cloned.1.call-start
  6.5 2.8 convert_element_type.33
  9.3 0.0 all-gather.3.cloned.1.call-update
  9.4 0.8 copy.13
  10.1 0.1 eq.29
  10.2 0.1 eq.25
  10.3 0.1 reshape_squeeze.3
  10.4 9.0 %reduce-window.6 = s32[32,8,128]{2,1,0:T(8,128)S(1)} reduce-window(s32[32,8,128]{2,1,0:T(8,128)S(1)} %fusion.21, s32[]{:T(128)} %constant.29.clone.1), window={size=1x1x128 pad=0_0x0_0x127_0}, to_apply=%region_0.0 | reduce-window | flops 4161536 | bytes 262148 | tf_op jit(solution)/shard_map/reduce-window
  19.5 0.1 slice.20
  19.6 0.1 copy.16
  19.7 0.1 copy.17
  19.8 0.1 broadcast_add_fusion
  20.0 0.0 copy-done.4
  20.0 0.1 multiply_reduce_fusion
  20.1 0.0 copy-done.3
  20.1 0.1 and_reduce_fusion
  20.2 4.3 %scatter_custom_fusion = s32[1152]{0:T(1024)S(1)} fusion(s32[1024]{0:T(1024)S(1)} %get-tuple-element.9, s32[1024]{0:T(1024)S(1)} %get-tuple-element.8, s32[]{:T(128)} %constant.28.clone.1), kind=kCustom, calls=%fused_computation.40 | custom fusion | bytes 4612
  24.5 0.1 reshape.93
  24.6 0.1 reshape.96
  24.7 0.0 copy-done.1
  24.8 6.0 %gather_fusion = bf16[1152,2048]{1,0:T(8,128)(2,1)} fusion(bf16[129,2048]{1,0:T(8,128)(2,1)S(1)} %concatenate.7, s32[2048]{0:T(1024)S(1)} %pad_clamp_fusion), kind=kCustom, calls=%fused_computation | custom fusion | bytes 9441792 | tf_op jit(solution)/shard_map/gather | solution.py:40
  30.8 7.2 %reshape.83 = bf16[32,1,36,2048]{3,2,0,1:T(8,128)(2,1)} reshape(bf16[1152,2048]{1,0:T(8,128)(2,1)} %gather_fusion) | data formatting | bytes 9437184 | tf_op jit(solution)/shard_map/reshape | solution.py:40
  38.0 0.0 copy-start
  38.0 8.1 %all-to-all-start = ((bf16[32,1,36,2048]{3,2,1,0:T(8,128)(2,1)}), bf16[32,1,36,2048]{3,2,1,0:T(8,128)(2,1)}, u32[]{:S(2)}, u32[]{:S(2)}) async-start(bf16[32,1,36,2048]{3,2,1,0:T(8,128)(2,1)} %bitcast.75), calls=%async_computation | async-start | bytes 10485760 | tf_op jit(solution)/shard_map/all_to_all | solution.py:41
  46.1 0.0 all-gather.5.cloned.1.call-start
  46.1 0.0 copy-done
  46.1 0.9 convert_element_type.35
  47.0 0.0 all-gather.5.cloned.1.call-update
  47.0 62.8 %all-to-all-done = bf16[32,1,36,2048]{3,2,1,0:T(8,128)(2,1)} async-done(((bf16[32,1,36,2048]{3,2,1,0:T(8,128)(2,1)}), bf16[32,1,36,2048]{3,2,1,0:T(8,128)(2,1)}, u32[]{:S(2)}, u32[]{:S(2)}) %all-to-all-start) | async-done | bytes 4718624 | tf_op jit(solution)/shard_map/all_to_all | solution.py:41
  109.9 0.0 all-gather.3.cloned.1.call-done
  109.9 17.5 %fusion.4 = f32[32,1,36,2048]{3,2,0,1:T(8,128)} fusion(bf16[1,2048,2048]{2,1,0:T(8,128)(2,1)} %all-gather.3.cloned.1.call-done, bf16[32,1,36,2048]{3,2,1,0:T(8,128)(2,1)} %all-to-all-done), kind=kOutput, calls=%fused_computation.9 | convolution fusion | flops 9663676416 | bytes 22544384 | tf_op jit(solution)/shard_map/secd,edf->secf/dot_general | solution.py:42
  127.4 34.5 %all-gather.5.cloned.1.call-done = bf16[1,1024,2048]{2,1,0:T(8,128)(2,1)} async-done(((bf16[1,128,2048]{2,1,0:T(8,128)(2,1)}), bf16[1,1024,2048]{2,1,0:T(8,128)(2,1)}) %all-gather.5.cloned.1.call-update) | async-done | bytes 4194320 | tf_op jit(solution)/shard_map/all_gather | solution.py:22
  161.8 11.3 %convert_bitcast_fusion = bf16[32,1,36,2048]{3,2,1,0:T(8,128)(2,1)} fusion(bf16[1,1024,2048]{2,1,0:T(8,128)(2,1)} %all-gather.5.cloned.1.call-done, f32[32,1,36,2048]{3,2,0,1:T(8,128)} %fusion.4), kind=kOutput, calls=%fused_computation.8 | convolution fusion | flops 4841275392 | bytes 18350080 | tf_op jit(solution)/shard_map/secf,efd->secd/dot_general | solution.py:46
  173.1 0.0 copy-start.2
  173.1 7.9 %all-to-all-start.1 = ((bf16[32,1,36,2048]{3,2,1,0:T(8,128)(2,1)}), bf16[32,1,36,2048]{3,2,1,0:T(8,128)(2,1)}, u32[]{:S(2)}, u32[]{:S(2)}) async-start(bf16[32,1,36,2048]{3,2,1,0:T(8,128)(2,1)} %convert_bitcast_fusion), calls=%async_computation.1 | async-start | bytes 10485760 | tf_op jit(solution)/shard_map/all_to_all | solution.py:50
  181.0 0.0 copy-done.2
  181.0 0.1 copy.21
  181.2 63.6 %all-to-all-done.1 = bf16[32,1,36,2048]{3,2,1,0:T(8,128)(2,1)} async-done(((bf16[32,1,36,2048]{3,2,1,0:T(8,128)(2,1)}), bf16[32,1,36,2048]{3,2,1,0:T(8,128)(2,1)}, u32[]{:S(2)}, u32[]{:S(2)}) %all-to-all-start.1) | async-done | bytes 4718624 | tf_op jit(solution)/shard_map/all_to_all | solution.py:50
  244.8 7.2 %copy.29 = bf16[32,1,36,2048]{3,0,2,1:T(8,128)(2,1)} copy(bf16[32,1,36,2048]{3,2,1,0:T(8,128)(2,1)} %all-to-all-done.1) | data formatting | bytes 9437184 | tf_op jit(solution)/shard_map/all_to_all | solution.py:50
  252.1 25.4 %gather_fusion.1 = bf16[1024,2048]{1,0:T(8,128)(2,1)} fusion(bf16[32,36,2048]{2,0,1:T(8,128)(2,1)} %bitcast.73, s32[1024]{0:T(1024)S(1)} %bitcast.74), kind=kCustom, calls=%fused_computation.1 | custom fusion | bytes 8396800 | tf_op jit(solution)/shard_map/gather | solution.py:52
  277.4 3.4 %fusion.9 = bf16[128,1,2048]{2,1,0:T(2,128)(2,1)S(1)} fusion(bf16[128,8,1]{1,2,0:T(2,128)(2,1)S(1)} %copy.21, bf16[1024,2048]{1,0:T(8,128)(2,1)} %gather_fusion.1), kind=kOutput, calls=%fused_computation.11 | convolution fusion | flops 4194304 | bytes 4720640 | tf_op jit(solution)/shard_map/tk,tkd->td/dot_general | solution.py:53
  280.8 1.1 copy.30
  (9 shorter events, 0.2 us)
Async XLA Ops:
  6.5 13.5 %copy-start.4 = (s32[2]{0:T(128)S(1)}, s32[2]{0:T(128)}, u32[]{:S(2)}) copy-start(s32[2]{0:T(128)} %constant.45) | copy-start | bytes 28
  6.5 13.5 %copy-start.3 = (s32[2]{0:T(128)S(1)}, s32[2]{0:T(128)}, u32[]{:S(2)}) copy-start(s32[2]{0:T(128)} %constant.48) | copy-start | bytes 28
  6.5 18.2 %copy-start.1 = (bf16[1,128,2048]{2,1,0:T(8,128)(2,1)S(1)}, bf16[1,128,2048]{2,1,0:T(8,128)(2,1)}, u32[]{:S(2)}) copy-start(bf16[1,128,2048]{2,1,0:T(8,128)(2,1)} %param.5) | copy-start | bytes 1572868
  6.5 103.3 %all-gather.3.cloned.1.call-start = ((), (), s32[]{:S(2)}) async-start(), calls=%async_computation.2 | async-start | bytes 9437184 | tf_op jit(solution)/shard_map/all_gather | solution.py:21
  38.0 8.1 %copy-start = (f32[1,128,2048]{2,1,0:T(8,128)S(1)}, f32[1,128,2048]{2,1,0:T(8,128)}, u32[]{:S(2)}) copy-start(f32[1,128,2048]{2,1,0:T(8,128)} %param.9) | copy-start | bytes 3145732
  38.0 71.9 %all-to-all-start = ((bf16[32,1,36,2048]{3,2,1,0:T(8,128)(2,1)}), bf16[32,1,36,2048]{3,2,1,0:T(8,128)(2,1)}, u32[]{:S(2)}, u32[]{:S(2)}) async-start(bf16[32,1,36,2048]{3,2,1,0:T(8,128)(2,1)} %bitcast.75), calls=%async_computation | async-start | bytes 10485760 | tf_op jit(solution)/shard_map/all_to_all | solution.py:41
  46.1 115.7 %all-gather.5.cloned.1.call-start = ((), (), s32[]{:S(2)}) async-start(), calls=%async_computation.3 | async-start | bytes 4718592 | tf_op jit(solution)/shard_map/all_gather | solution.py:22
  173.1 7.9 %copy-start.2 = (f32[1,128,8]{1,2,0:T(8,128)S(1)}, f32[1,128,8]{1,2,0:T(8,128)}, u32[]{:S(2)}) copy-start(f32[1,128,8]{1,2,0:T(8,128)} %param.7) | copy-start | bytes 12292
  173.1 71.7 %all-to-all-start.1 = ((bf16[32,1,36,2048]{3,2,1,0:T(8,128)(2,1)}), bf16[32,1,36,2048]{3,2,1,0:T(8,128)(2,1)}, u32[]{:S(2)}, u32[]{:S(2)}) async-start(bf16[32,1,36,2048]{3,2,1,0:T(8,128)(2,1)} %convert_bitcast_fusion), calls=%async_computation.1 | async-start | bytes 10485760 | tf_op jit(solution)/shard_map/all_to_all | solution.py:50
Sparse Core Ops, SparseCore 0:
  9.5 96.9 all-gather.2
  108.3 53.4 all-gather.4
where the time goes:
time: 290 us; the launch traced here: 289 us
  waiting for transfers between devices  161 us (56%)
  local copies, waits for them, and re-layouts  53 us (18%)
  matrix products  32.2 us (11%)
  starting transfers between devices  16 us (6%)
  between operations  13.6 us (5%)
  other arithmetic  13.1 us (5%)
    all_to_all x1, waiting for transfers between devices, per_device(): lax.all_to_all(expert_out, 'tok', split_axis=0, concat_axis=0, tiled=True)  63.6 us
    all_to_all x1, waiting for transfers between devices, per_device(): lax.all_to_all(send_rows, 'tok', split_axis=0, concat_axis=0, tiled=True)  62.8 us
    all_gather x1, waiting for transfers between devices, per_device(): lax.all_gather(served_down, 'rep', axis=1, tiled=True)  34.5 us
    gather x1, local copies, waits for them, and re-layouts, per_device(): returned[flat_picks, slot_index]  25.4 us
    dot_general x1, matrix products, per_device(): jnp.einsum('secd,edf->secf', arrived, full_gate, preferred_element_type=j...  17.5 us
    dot_general x1, matrix products, per_device(): jnp.einsum('secf,efd->secd', hidden_units, full_down, preferred_element_t...  11.3 us
    another operation x3, other arithmetic  9.15 us
    all_to_all x1, starting transfers between devices, per_device(): lax.all_to_all(send_rows, 'tok', split_axis=0, concat_axis=0, tiled=True)  8.06 us
  transfers between devices with their start and end apart: 4, of which 3 were waited for; matrix products, arithmetic and copies ran while one was open for 16% of the time, Pallas kernels for 0%

commit v1 on v0

--- a/solution.py
+++ b/solution.py
@@ -19,7 +19,9 @@
     unit_count = served_gate.shape[2] // 2
     full_gate, full_down = (
         lax.all_gather(served_gate, "rep", axis=1, tiled=True),
-        lax.all_gather(served_down, "rep", axis=1, tiled=True),
+        jnp.concatenate(
+            lax.all_to_all(jnp.stack([served_down] * lax.axis_size("rep")), "rep", 0, 0), axis=1
+        ),
     )
     flat_picks = routes[0].reshape(-1)
     pick_count = flat_picks.shape[0]

time: 290 us -> 343 us (1.18)
  waiting for transfers between devices: 161 us -> 205 us
  starting transfers between devices: 16 us -> 22.7 us
    all_to_all x0 -> x1, waiting for transfers between devices: none -> 78.1 us  [per_device(): lax.all_to_all(jnp.stack([served_down] * lax.axis_size('rep')), 'rep', 0, 0)]
    all_gather x1 -> x0, waiting for transfers between devices: 34.5 us -> none  [per_device(): lax.all_gather(served_down, 'rep', axis=1, tiled=True)]
    all_to_all x0 -> x1, starting transfers between devices: none -> 8.19 us  [per_device(): lax.all_to_all(jnp.stack([served_down] * lax.axis_size('rep')), 'rep', 0, 0)]
  transfers between devices with their start and end apart: 4 -> 4, of which waited for: 3 -> 3; matrix products, arithmetic and copies ran while one was open for 16% -> 14% of each run, Pallas kernels for 0% -> 0%
where the time goes in v1:
time: 343 us; the launch traced here: 342 us
  waiting for transfers between devices  205 us (60%)
  local copies, waits for them, and re-layouts  55.6 us (16%)
  matrix products  32.1 us (9%)
  starting transfers between devices  22.7 us (7%)
  between operations  13.6 us (4%)
  other arithmetic  12.3 us (4%)
    all_to_all x1, waiting for transfers between devices, per_device(): lax.all_to_all(jnp.stack([served_down] * lax.axis_size('rep')), 'rep', 0, 0)  78.1 us
    all_to_all x1, waiting for transfers between devices, per_device(): lax.all_to_all(send_rows, 'tok', split_axis=0, concat_axis=0, tiled=True)  63.7 us
    all_to_all x1, waiting for transfers between devices, per_device(): lax.all_to_all(expert_out, 'tok', split_axis=0, concat_axis=0, tiled=True)  63.6 us
    gather x1, local copies, waits for them, and re-layouts, per_device(): returned[flat_picks, slot_index]  25.4 us
    dot_general x1, matrix products, per_device(): jnp.einsum('secd,edf->secf', arrived, full_gate, preferred_element_type=j...  17.4 us
    dot_general x1, matrix products, per_device(): jnp.einsum('secf,efd->secd', hidden_units, full_down, preferred_element_t...  11.3 us
    another operation x3, other arithmetic  9.15 us
    all_to_all x1, starting transfers between devices, per_device(): lax.all_to_all(jnp.stack([served_down] * lax.axis_size('rep')), 'rep', 0, 0)  8.19 us
  transfers between devices with their start and end apart: 4, of which 3 were waited for; matrix products, arithmetic and copies ran while one was open for 14% of the time, Pallas kernels for 0%

profile of v1, /device:TPU:7, one launch (start us, length us, event | category | flops | bytes accessed | tf_op | source)
XLA Modules:
  0.0 341.7 jit_solution(3079459023881840418)
XLA Ops:
  6.5 0.0 copy-start.4
  6.5 0.0 copy-start.3
  6.5 0.0 copy-start.1
  6.5 0.0 all-gather.2.cloned.1.call-start
  6.5 2.8 convert_element_type.35
  9.3 0.0 all-gather.2.cloned.1.call-update
  9.4 0.8 copy.13
  10.2 0.1 eq.29
  10.3 0.1 eq.25
  10.3 0.1 reshape_squeeze.3
  10.5 9.0 %reduce-window.6 = s32[32,8,128]{2,1,0:T(8,128)S(1)} reduce-window(s32[32,8,128]{2,1,0:T(8,128)S(1)} %fusion.17, s32[]{:T(128)} %constant.29.clone.1), window={size=1x1x128 pad=0_0x0_0x127_0}, to_apply=%region_0.0 | reduce-window | flops 4161536 | bytes 262148 | tf_op jit(solution)/shard_map/reduce-window
  19.5 0.1 slice.20
  19.6 0.1 copy.16
  19.7 0.1 copy.17
  19.8 0.1 broadcast_add_fusion
  20.0 0.0 copy-done.4
  20.0 0.1 multiply_reduce_fusion
  20.1 0.0 copy-done.3
  20.1 0.1 and_reduce_fusion
  20.2 4.3 %scatter_custom_fusion = s32[1152]{0:T(1024)S(1)} fusion(s32[1024]{0:T(1024)S(1)} %get-tuple-element.9, s32[1024]{0:T(1024)S(1)} %get-tuple-element.8, s32[]{:T(128)} %constant.28.clone.1), kind=kCustom, calls=%fused_computation.39 | custom fusion | bytes 4612
  24.5 0.1 reshape.98
  24.7 0.1 reshape.101
  24.8 0.0 copy-done.1
  24.8 6.0 %gather_fusion = bf16[1152,2048]{1,0:T(8,128)(2,1)} fusion(bf16[129,2048]{1,0:T(8,128)(2,1)S(1)} %concatenate.7, s32[2048]{0:T(1024)S(1)} %pad_clamp_fusion), kind=kCustom, calls=%fused_computation | custom fusion | bytes 9441792 | tf_op jit(solution)/shard_map/gather | solution.py:42
  30.8 7.2 %reshape.88 = bf16[32,1,36,2048]{3,2,0,1:T(8,128)(2,1)} reshape(bf16[1152,2048]{1,0:T(8,128)(2,1)} %gather_fusion) | data formatting | bytes 9437184 | tf_op jit(solution)/shard_map/reshape | solution.py:42
  38.0 0.0 copy-start
  38.0 8.1 %all-to-all-start = ((bf16[32,1,36,2048]{3,2,1,0:T(8,128)(2,1)}), bf16[32,1,36,2048]{3,2,1,0:T(8,128)(2,1)}, u32[]{:S(2)}, u32[]{:S(2)}) async-start(bf16[32,1,36,2048]{3,2,1,0:T(8,128)(2,1)} %bitcast.75), calls=%async_computation | async-start | bytes 10485760 | tf_op jit(solution)/shard_map/all_to_all | solution.py:43
  46.1 0.0 copy-done
  46.1 0.1 convert_bitcast_fusion.1
  46.2 63.7 %all-to-all-done = bf16[32,1,36,2048]{3,2,1,0:T(8,128)(2,1)} async-done(((bf16[32,1,36,2048]{3,2,1,0:T(8,128)(2,1)}), bf16[32,1,36,2048]{3,2,1,0:T(8,128)(2,1)}, u32[]{:S(2)}, u32[]{:S(2)}) %all-to-all-start) | async-done | bytes 4718624 | tf_op jit(solution)/shard_map/all_to_all | solution.py:43
  109.9 2.6 stack.2
  112.5 8.2 %all-to-all-start.1 = ((bf16[8,1,128,2048]{3,2,1,0:T(8,128)(2,1)}), bf16[8,1,128,2048]{3,2,1,0:T(8,128)(2,1)}, u32[]{:S(2)}, u32[]{:S(2)}) async-start(bf16[8,1,128,2048]{3,2,1,0:T(8,128)(2,1)} %stack.2), calls=%async_computation.1 | async-start | bytes 8388608 | tf_op jit(solution)/shard_map/all_to_all | solution.py:23
  120.7 0.0 all-gather.2.cloned.1.call-done
  120.7 17.4 %fusion.4 = f32[32,1,36,2048]{3,2,0,1:T(8,128)} fusion(bf16[1,2048,2048]{2,1,0:T(8,128)(2,1)} %all-gather.2.cloned.1.call-done, bf16[32,1,36,2048]{3,2,1,0:T(8,128)(2,1)} %all-to-all-done), kind=kOutput, calls=%fused_computation.9 | convolution fusion | flops 9663676416 | bytes 22544384 | tf_op jit(solution)/shard_map/secd,edf->secf/dot_general | solution.py:44
  138.1 78.1 %all-to-all-done.1 = bf16[8,1,128,2048]{3,2,1,0:T(8,128)(2,1)} async-done(((bf16[8,1,128,2048]{3,2,1,0:T(8,128)(2,1)}), bf16[8,1,128,2048]{3,2,1,0:T(8,128)(2,1)}, u32[]{:S(2)}, u32[]{:S(2)}) %all-to-all-start.1) | async-done | bytes 4194336 | tf_op jit(solution)/shard_map/all_to_all | solution.py:23
  216.2 11.3 %convert_bitcast_fusion = bf16[32,1,36,2048]{3,2,1,0:T(8,128)(2,1)} fusion(bf16[1024,2048,1]{1,0,2:T(8,128)(2,1)} %bitcast.16, f32[32,1,36,2048]{3,2,0,1:T(8,128)} %fusion.4), kind=kOutput, calls=%fused_computation.8 | convolution fusion | flops 4841275392 | bytes 18350080 | tf_op jit(solution)/shard_map/secf,efd->secd/dot_general | solution.py:48
  227.5 0.0 copy-start.2
  227.5 6.4 %all-to-all-start.2 = ((bf16[32,1,36,2048]{3,2,1,0:T(8,128)(2,1)}), bf16[32,1,36,2048]{3,2,1,0:T(8,128)(2,1)}, u32[]{:S(2)}, u32[]{:S(2)}) async-start(bf16[32,1,36,2048]{3,2,1,0:T(8,128)(2,1)} %convert_bitcast_fusion), calls=%async_computation.2 | async-start | bytes 10485760 | tf_op jit(solution)/shard_map/all_to_all | solution.py:52
  233.9 0.0 copy-done.2
  234.0 0.1 copy.21
  234.1 63.6 %all-to-all-done.2 = bf16[32,1,36,2048]{3,2,1,0:T(8,128)(2,1)} async-done(((bf16[32,1,36,2048]{3,2,1,0:T(8,128)(2,1)}), bf16[32,1,36,2048]{3,2,1,0:T(8,128)(2,1)}, u32[]{:S(2)}, u32[]{:S(2)}) %all-to-all-start.2) | async-done | bytes 4718624 | tf_op jit(solution)/shard_map/all_to_all | solution.py:52
  297.7 7.2 %copy.29 = bf16[32,1,36,2048]{3,0,2,1:T(8,128)(2,1)} copy(bf16[32,1,36,2048]{3,2,1,0:T(8,128)(2,1)} %all-to-all-done.2) | data formatting | bytes 9437184 | tf_op jit(solution)/shard_map/all_to_all | solution.py:52
  305.0 25.4 %gather_fusion.1 = bf16[1024,2048]{1,0:T(8,128)(2,1)} fusion(bf16[32,36,2048]{2,0,1:T(8,128)(2,1)} %bitcast.73, s32[1024]{0:T(1024)S(1)} %bitcast.74), kind=kCustom, calls=%fused_computation.1 | custom fusion | bytes 8396800 | tf_op jit(solution)/shard_map/gather | solution.py:54
  330.4 3.4 fusion.9
  333.8 1.1 copy.30
  (9 shorter events, 0.2 us)
Async XLA Ops:
  6.5 13.5 %copy-start.4 = (s32[2]{0:T(128)S(1)}, s32[2]{0:T(128)}, u32[]{:S(2)}) copy-start(s32[2]{0:T(128)} %constant.45) | copy-start | bytes 28
  6.5 13.6 %copy-start.3 = (s32[2]{0:T(128)S(1)}, s32[2]{0:T(128)}, u32[]{:S(2)}) copy-start(s32[2]{0:T(128)} %constant.48) | copy-start | bytes 28
  6.5 18.2 %copy-start.1 = (bf16[1,128,2048]{2,1,0:T(8,128)(2,1)S(1)}, bf16[1,128,2048]{2,1,0:T(8,128)(2,1)}, u32[]{:S(2)}) copy-start(bf16[1,128,2048]{2,1,0:T(8,128)(2,1)} %param.5) | copy-start | bytes 1572868
  6.5 114.1 %all-gather.2.cloned.1.call-start = ((), (), s32[]{:S(2)}) async-start(), calls=%async_computation.3 | async-start | bytes 9437184 | tf_op jit(solution)/shard_map/all_gather | solution.py:21
  38.0 8.1 %copy-start = (f32[1,128,2048]{2,1,0:T(8,128)S(1)}, f32[1,128,2048]{2,1,0:T(8,128)}, u32[]{:S(2)}) copy-start(f32[1,128,2048]{2,1,0:T(8,128)} %param.9) | copy-start | bytes 3145732
  38.0 71.9 %all-to-all-start = ((bf16[32,1,36,2048]{3,2,1,0:T(8,128)(2,1)}), bf16[32,1,36,2048]{3,2,1,0:T(8,128)(2,1)}, u32[]{:S(2)}, u32[]{:S(2)}) async-start(bf16[32,1,36,2048]{3,2,1,0:T(8,128)(2,1)} %bitcast.75), calls=%async_computation | async-start | bytes 10485760 | tf_op jit(solution)/shard_map/all_to_all | solution.py:43
  112.5 103.7 %all-to-all-start.1 = ((bf16[8,1,128,2048]{3,2,1,0:T(8,128)(2,1)}), bf16[8,1,128,2048]{3,2,1,0:T(8,128)(2,1)}, u32[]{:S(2)}, u32[]{:S(2)}) async-start(bf16[8,1,128,2048]{3,2,1,0:T(8,128)(2,1)} %stack.2), calls=%async_computation.1 | async-start | bytes 8388608 | tf_op jit(solution)/shard_map/all_to_all | solution.py:23
  227.5 6.5 %copy-start.2 = (f32[1,128,8]{1,2,0:T(8,128)S(1)}, f32[1,128,8]{1,2,0:T(8,128)}, u32[]{:S(2)}) copy-start(f32[1,128,8]{1,2,0:T(8,128)} %param.7) | copy-start | bytes 12292
  227.5 70.2 %all-to-all-start.2 = ((bf16[32,1,36,2048]{3,2,1,0:T(8,128)(2,1)}), bf16[32,1,36,2048]{3,2,1,0:T(8,128)(2,1)}, u32[]{:S(2)}, u32[]{:S(2)}) async-start(bf16[32,1,36,2048]{3,2,1,0:T(8,128)(2,1)} %convert_bitcast_fusion), calls=%async_computation.2 | async-start | bytes 10485760 | tf_op jit(solution)/shard_map/all_to_all | solution.py:52
Sparse Core Ops, SparseCore 0:
  9.5 96.9 all-gather.1
